TPU v7x, 32 devices: a whole 2x2x4 slice. The times are simulated.
32 devices in a mesh: item: 8 (over z, y), code: 4 (over x, core).
Axes of the slice: x: 2, y: 2, z: 4, core: 2. Of those that a mesh axis runs over, the one named last changes fastest.
Arguments:
- residuals: float32 [256, 32768], P('code', 'item'), may hold values from -6 to 6
- codebook: float32 [256, 32768], P('item', 'code'), may hold values from -6 to 6
- item_weight: float32 [32768], P('item'), may hold values from 1 to 100
- code_capacity: float32 [32768], P('code'), may hold values from 0.25 to 4
- pairs: int32 [512, 64], P('item', 'code'), may hold values from -1 to 127, as said below
Outputs:
- item_potential: float32 [32768], P('item')
- code_potential: float32 [32768], P('code')
Inputs may be any that keep to these rules, and one draw needn't show every extreme that they name: `pairs`: each entry is -1 (no candidate) or a code block's number within the code shard of its slot column. Within one item block and one code shard the live entries are distinct, the first slot is always live, and between 1 and 8 are live; some device holds exactly 8 live slots in every item block. Every code block is named by some item block.
All inputs are finite; a program needn't handle non-finite values.
Results may differ from a plain program's by a relative error of at most 0.0003.
Values sent between devices are 32-bit elements; how exact they have to be, the bound alone decides.
No kernel may reach another device: no remote copies, remote signals or barrier semaphores. Data moves between devices by JAX's collectives and lax.ppermute only.
A program may use at most 128 MiB of HBM per device.

v0:
```python
import math

import jax
import jax.numpy as jnp
from jax import lax
from jax.sharding import PartitionSpec as P

BLOCK = 64
ITERS = 3


masked_score = -1e30
softness_factor = 0.1


def body(residuals, codebook, item_weight, code_capacity, pairs):
    item_columns = lax.all_gather(residuals, "code", axis=0, tiled=True)
    code_cols = lax.all_gather(codebook, "item", axis=0, tiled=True)
    embedding_width = item_columns.shape[0]
    item_count = item_columns.shape[1]
    code_count = code_cols.shape[1]
    item_blocks = item_count // BLOCK
    code_blocks = code_count // BLOCK
    logit_scale = 1.0 / (softness_factor * math.sqrt(embedding_width))
    weight_sum = lax.psum(jnp.sum(item_weight), "item")
    capacity_sum = lax.psum(jnp.sum(code_capacity), "code")
    item_logmass = jnp.log(item_weight) - jnp.log(weight_sum)
    code_logmass = jnp.log(code_capacity) - jnp.log(capacity_sum)
    slot_order = jnp.argsort((pairs < 0).astype(jnp.int32), axis=1, stable=True)[
        :, : pairs.shape[1] // 2
    ]
    chosen = jnp.take_along_axis(pairs, slot_order, axis=1)
    is_live = chosen >= 0
    safe_ids = jnp.where(is_live, chosen, 0)
    target = jnp.where(is_live, chosen, code_blocks)
    item_split_cols = item_columns.reshape(embedding_width, item_blocks, BLOCK)
    code_column_splits = code_cols.reshape(embedding_width, code_blocks, BLOCK)
    group = math.gcd(item_blocks, 8)
    group_count = item_blocks // group

    def build_tiles(own, ids, live):
        picked = code_column_splits[:, ids, :]
        scores = (
            jnp.einsum("rbi,rbsj->bsij", own, picked, precision=lax.Precision.HIGHEST) * logit_scale
        )
        return jnp.where(live[:, :, None, None], scores, masked_score)

    reduce_fn = lambda tiles, ids, portion: tiles

    def one_group(group_index):
        start = group_index * group
        own = lax.dynamic_slice_in_dim(item_split_cols, start, group, 1)
        ids = lax.dynamic_slice_in_dim(safe_ids, start, group, 0)
        live = lax.dynamic_slice_in_dim(is_live, start, group, 0)
        portion = lax.dynamic_slice_in_dim(safe_ids, start, group, 0)
        return reduce_fn(build_tiles(own, ids, live), ids, portion)

    results = lax.map(one_group, jnp.arange(group_count, dtype=jnp.int32))
    saved_tile_blocks = results.reshape((item_blocks,) + results.shape[2:])

    def run_pass(reduce_fn, extra):
        return reduce_fn(saved_tile_blocks, safe_ids, extra)

    flat_target = target.reshape(-1)
    flat_rows = flat_target.shape[0]
    row_group = math.gcd(flat_rows, 256)
    one_hot = flat_target[:, None] == jnp.arange(code_blocks, dtype=jnp.int32)[None, :]
    one_hot_groups = one_hot.reshape(flat_rows // row_group, row_group, code_blocks)
    one_hot_float = one_hot.astype(jnp.float32)
    code_potential = jnp.zeros((code_count,), jnp.float32)
    item_potential = jnp.zeros((item_count,), jnp.float32)
    for sweep in range(ITERS):
        code_split = code_potential.reshape(code_blocks, BLOCK)

        def row_reduce(tiles, ids, portion):
            logits = tiles + code_split[ids][:, :, None, :]
            block_peak = jnp.max(logits, axis=(1, 3))
            block_total = jnp.sum(jnp.exp(logits - block_peak[:, None, :, None]), axis=(1, 3))
            return (block_peak, block_total)

        row_peak, row_total = run_pass(row_reduce, safe_ids)
        row_peak = row_peak.reshape(item_count)
        row_total = row_total.reshape(item_count)
        merged_peak = lax.pmax(row_peak, "code")
        merged_total = lax.psum(row_total * jnp.exp(row_peak - merged_peak), "code")
        item_potential = item_logmass - (merged_peak + jnp.log(merged_total))
        item_split = item_potential.reshape(item_blocks, BLOCK)

        def col_reduce(tiles, ids, portion):
            logits = tiles + portion[:, None, :, None]
            block_peak = jnp.max(logits, axis=2)
            block_total = jnp.sum(jnp.exp(logits - block_peak[:, :, None, :]), axis=2)
            return (block_peak, block_total)

        tile_peak, tile_total = run_pass(col_reduce, item_split)
        peak_flat = tile_peak.reshape(flat_rows, BLOCK)
        total_flat = tile_total.reshape(flat_rows, BLOCK)
        peak_groups = peak_flat.reshape(flat_rows // row_group, row_group, BLOCK)

        def peak_step(carry, pieces):
            hot, peaks = pieces
            candidate = jnp.max(jnp.where(hot[:, :, None], peaks[:, None, :], masked_score), axis=0)
            return (jnp.maximum(carry, candidate), None)

        col_peak, unused = lax.scan(
            peak_step,
            jnp.full((code_blocks, BLOCK), masked_score, jnp.float32),
            (one_hot_groups, peak_groups),
        )
        padded_peak = jnp.concatenate(
            [col_peak, jnp.full((1, BLOCK), masked_score, jnp.float32)], axis=0
        )
        spread = total_flat * jnp.exp(peak_flat - padded_peak[flat_target])
        col_total = jnp.dot(
            one_hot_float.T,
            spread,
            precision=lax.Precision.HIGHEST,
            preferred_element_type=jnp.float32,
        )
        col_peak = col_peak.reshape(code_count)
        col_total = col_total.reshape(code_count)
        joined_peak = lax.pmax(col_peak, "item")
        joined_total = lax.psum(col_total * jnp.exp(col_peak - joined_peak), "item")
        code_potential = code_logmass - (joined_peak + jnp.log(joined_total))
    return (item_potential, code_potential)


def solution(mesh):
    placed = (P("code", "item"), P("item", "code"), P("item"), P("code"), P("item", "code"))
    return jax.shard_map(
        body, mesh=mesh, in_specs=placed, out_specs=(P("item"), P("code")), check_vma=False
    )
```

profile of v0, /device:TPU:0, one launch (start us, length us, event | category | flops | bytes accessed | tf_op | source)
XLA Modules:
  0.0 706.6 jit_solution(5821192888771860012)
XLA Ops:
  10.0 23.8 %psum.56 = f32[]{:T(128)} all-reduce(f32[]{:T(128)} %reduce_sum.72), channel_id=1, replica_groups=mesh['item'=8,'code'=4] {'item'}, use_global_device_ids=true, to_apply=%region_1.0 | all-reduce | flops 1 | bytes 8 | tf_op jit(solution)/shard_map/psum | solution.py:25
  52.4 121.0 %all-gather.3.cloned.1.call-done = f32[256,8192]{1,0:T(8,128)} async-done(((f32[32,8192]{1,0:T(8,128)}), f32[256,8192]{1,0:T(8,128)}) %all-gather.3.cloned.1.call-update) | async-done | bytes 8388624 | tf_op jit(solution)/shard_map/all_gather | solution.py:18
  173.4 9.0 %copy.37 = f32[256,8192]{0,1:T(8,128)} copy(f32[256,8192]{1,0:T(8,128)} %all-gather.3.cloned.1.call-done) | data formatting | bytes 16777216 | tf_op jit(solution)/shard_map/all_gather | solution.py:18
  182.4 120.6 %while.43 = (s32[]{:T(128)}, f32[8,8,8,64,64]{3,4,2,1,0:T(8,128)}, s32[8]{0:T(128)S(1)}, pred[64,8]{0,1:T(8,128)(4,1)S(1)}, s32[64,8]{0,1:T(8,128)S(1)}, /*index...) while((s32[]{:T(128)}, f32[8,8,8,64,64]{3,4,2,1,0:T(8,128)}, ...), condition=%wide.region_4.0_spmd, body=%wide.region_3.0_spmd.sunk | while | flops 805831872 | bytes 15212019 | solution.py:58
  190.2 7.3 %bitcast_dynamic-update-slice_fusion.2 = f32[8,8,8,64,64]{3,4,2,1,0:T(8,128)} fusion(f32[8,8,8,64,64]{3,4,2,1,0:T(8,128)} %get-tuple-element.349, s32[]{:T(128)} %get-tuple-element.348, f32[256,8,8,64]{0,3,2,1:T(8,128)} %bitcast.88, pred[8,8]{1,0:T(8,128)(4,1)S(1)} %copy.63, f32[256,64,64]{0,2,1:T(8,128)} %get-tuple-element.365, s32[]{:T(128)S(6)} %select_n.148), kind=kOutput, calls=%fused_computation.8.clone.1 | convolution fusion | flops 805830656 | bytes 6816324 | tf_op jit(solution)/shard_map/while/body/eval_jaxpr/rbi,rbsj->bsij/dot_general | solution.py:44
  235.4 7.3 %bitcast_dynamic-update-slice_fusion.2 = f32[8,8,8,64,64]{3,4,2,1,0:T(8,128)} fusion(f32[8,8,8,64,64]{3,4,2,1,0:T(8,128)} %get-tuple-element.349, s32[]{:T(128)} %get-tuple-element.348, f32[256,8,8,64]{0,3,2,1:T(8,128)} %bitcast.88, pred[8,8]{1,0:T(8,128)(4,1)S(1)} %copy.63, f32[256,64,64]{0,2,1:T(8,128)} %get-tuple-element.365, s32[]{:T(128)S(6)} %select_n.148), kind=kOutput, calls=%fused_computation.8.clone.1 | convolution fusion | flops 805830656 | bytes 6816324 | tf_op jit(solution)/shard_map/while/body/eval_jaxpr/rbi,rbsj->bsij/dot_general | solution.py:44
  250.4 7.3 %bitcast_dynamic-update-slice_fusion.2 = f32[8,8,8,64,64]{3,4,2,1,0:T(8,128)} fusion(f32[8,8,8,64,64]{3,4,2,1,0:T(8,128)} %get-tuple-element.349, s32[]{:T(128)} %get-tuple-element.348, f32[256,8,8,64]{0,3,2,1:T(8,128)} %bitcast.88, pred[8,8]{1,0:T(8,128)(4,1)S(1)} %copy.63, f32[256,64,64]{0,2,1:T(8,128)} %get-tuple-element.365, s32[]{:T(128)S(6)} %select_n.148), kind=kOutput, calls=%fused_computation.8.clone.1 | convolution fusion | flops 805830656 | bytes 6816324 | tf_op jit(solution)/shard_map/while/body/eval_jaxpr/rbi,rbsj->bsij/dot_general | solution.py:44
  280.6 7.3 %bitcast_dynamic-update-slice_fusion.2 = f32[8,8,8,64,64]{3,4,2,1,0:T(8,128)} fusion(f32[8,8,8,64,64]{3,4,2,1,0:T(8,128)} %get-tuple-element.349, s32[]{:T(128)} %get-tuple-element.348, f32[256,8,8,64]{0,3,2,1:T(8,128)} %bitcast.88, pred[8,8]{1,0:T(8,128)(4,1)S(1)} %copy.63, f32[256,64,64]{0,2,1:T(8,128)} %get-tuple-element.365, s32[]{:T(128)S(6)} %select_n.148), kind=kOutput, calls=%fused_computation.8.clone.1 | convolution fusion | flops 805830656 | bytes 6816324 | tf_op jit(solution)/shard_map/while/body/eval_jaxpr/rbi,rbsj->bsij/dot_general | solution.py:44
  295.7 7.3 %bitcast_dynamic-update-slice_fusion.2 = f32[8,8,8,64,64]{3,4,2,1,0:T(8,128)} fusion(f32[8,8,8,64,64]{3,4,2,1,0:T(8,128)} %get-tuple-element.349, s32[]{:T(128)} %get-tuple-element.348, f32[256,8,8,64]{0,3,2,1:T(8,128)} %bitcast.88, pred[8,8]{1,0:T(8,128)(4,1)S(1)} %copy.63, f32[256,64,64]{0,2,1:T(8,128)} %get-tuple-element.365, s32[]{:T(128)S(6)} %select_n.148), kind=kOutput, calls=%fused_computation.8.clone.1 | convolution fusion | flops 805830656 | bytes 6816324 | tf_op jit(solution)/shard_map/while/body/eval_jaxpr/rbi,rbsj->bsij/dot_general | solution.py:44
  302.9 9.4 %add_reduce_fusion.5 = f32[8,8,64]{2,1,0:T(8,128)S(1)} fusion(f32[8,8,8,64,64]{3,4,2,1,0:T(8,128)} %get-tuple-element.107, f32[8,8,8,64]{3,2,1,0:T(8,128)S(1)} %bitcast.97), kind=kLoop, calls=%fused_computation.39 | loop fusion | flops 4190208 | bytes 8536064 | tf_op jit(solution)/shard_map/reduce_max | solution.py:77
  319.0 10.2 %pmax.42 = f32[4096]{0:T(1024)S(1)} all-reduce(f32[4096]{0:T(1024)S(1)} %reshape.247), channel_id=1, replica_groups=mesh['item'=8,'code'=4] {'code'}, use_global_device_ids=true, to_apply=%region_8.9 | all-reduce | flops 4096 | bytes 32768 | tf_op jit(solution)/shard_map/pmax | solution.py:84
  329.2 11.4 %all-reduce.3 = (f32[4096]{0:T(1024)S(1)}, f32[]{:T(128)}) all-reduce(f32[4096]{0:T(1024)S(1)} %exponential_multiply_fusion.5, f32[]{:T(128)} %reduce_sum.73), channel_id=1, replica_groups=mesh['item'=8,'code'=4] {'code'}, use_global_device_ids=true, to_apply=%region_10.11 | all-reduce | flops 4097 | bytes 32776 | tf_op jit(solution)/shard_map/psum | solution.py:85
  340.7 8.2 %add_reduce_fusion.4 = f32[8,8,8,64]{3,2,1,0:T(8,128)S(1)} fusion(f32[8,8,8,64,64]{3,4,2,1,0:T(8,128)} %get-tuple-element.107, f32[8,8,64]{2,1,0:T(8,128)S(1)} %add.166), kind=kLoop, calls=%fused_computation.38 | loop fusion | flops 4161536 | bytes 8536064 | tf_op jit(solution)/shard_map/reduce_max | solution.py:91
  348.9 11.1 %exponential_reduce_fusion.4 = f32[8,8,8,64]{3,2,1,0:T(8,128)S(1)} fusion(f32[8,8,8,64,64]{3,4,2,1,0:T(8,128)} %get-tuple-element.107, f32[8,8,8,64]{3,2,1,0:T(8,128)S(1)} %add_reduce_fusion.4, f32[8,8,64]{2,1,0:T(8,128)S(1)} %add.166), kind=kLoop, calls=%fused_computation.32 | loop fusion | flops 6258688 | bytes 8667136 | tf_op jit(solution)/shard_map/reduce_sum | solution.py:92
  368.5 35.2 %pmax.43 = f32[8192]{0:T(1024)S(1)} all-reduce(f32[8192]{0:T(1024)S(1)} %reshape.249), channel_id=1, replica_groups=mesh['item'=8,'code'=4] {'item'}, use_global_device_ids=true, to_apply=%region_15.16 | all-reduce | flops 8192 | bytes 65536 | tf_op jit(solution)/shard_map/pmax | solution.py:122
  403.7 33.0 %psum.59 = f32[8192]{0:T(1024)S(1)} all-reduce(f32[8192]{0:T(1024)S(1)} %exponential_multiply_fusion.2), channel_id=1, replica_groups=mesh['item'=8,'code'=4] {'item'}, use_global_device_ids=true, to_apply=%region_17.18 | all-reduce | flops 8192 | bytes 65536 | tf_op jit(solution)/shard_map/psum | solution.py:123
  438.6 7.6 %add_reduce_fusion.3 = f32[8,8,64]{2,1,0:T(8,128)S(1)} fusion(f32[8,8,8,64,64]{3,4,2,1,0:T(8,128)} %get-tuple-element.107, f32[8,8,8,64]{3,2,1,0:T(8,128)S(1)} %bitcast.101), kind=kLoop, calls=%fused_computation.37 | loop fusion | flops 4190208 | bytes 8536064 | tf_op jit(solution)/shard_map/reduce_max | solution.py:77
  446.2 7.6 %exponential_reduce_fusion.3 = f32[8,8,64]{2,1,0:T(8,128)S(1)} fusion(f32[8,8,8,64,64]{3,4,2,1,0:T(8,128)} %get-tuple-element.107, f32[8,8,64]{2,1,0:T(8,128)S(1)} %add_reduce_fusion.3, f32[8,8,8,64]{3,2,1,0:T(8,128)S(1)} %bitcast.102), kind=kLoop, calls=%fused_computation.31 | loop fusion | flops 6287360 | bytes 8552448 | tf_op jit(solution)/shard_map/reduce_sum | solution.py:78
  454.0 10.1 %pmax.44 = f32[4096]{0:T(1024)S(1)} all-reduce(f32[4096]{0:T(1024)S(1)} %reshape.254), channel_id=1, replica_groups=mesh['item'=8,'code'=4] {'code'}, use_global_device_ids=true, to_apply=%region_19.20 | all-reduce | flops 4096 | bytes 32768 | tf_op jit(solution)/shard_map/pmax | solution.py:84
  464.1 10.1 %psum.60 = f32[4096]{0:T(1024)S(1)} all-reduce(f32[4096]{0:T(1024)S(1)} %exponential_multiply_fusion.4), channel_id=1, replica_groups=mesh['item'=8,'code'=4] {'code'}, use_global_device_ids=true, to_apply=%region_21.22 | all-reduce | flops 4096 | bytes 32768 | tf_op jit(solution)/shard_map/psum | solution.py:85
  474.3 8.2 %add_reduce_fusion.2 = f32[8,8,8,64]{3,2,1,0:T(8,128)S(1)} fusion(f32[8,8,8,64,64]{3,4,2,1,0:T(8,128)} %get-tuple-element.107, f32[8,8,64]{2,1,0:T(8,128)S(1)} %add.175), kind=kLoop, calls=%fused_computation.36 | loop fusion | flops 4161536 | bytes 8536064 | tf_op jit(solution)/shard_map/reduce_max | solution.py:91
  482.5 11.1 %exponential_reduce_fusion.2 = f32[8,8,8,64]{3,2,1,0:T(8,128)S(1)} fusion(f32[8,8,8,64,64]{3,4,2,1,0:T(8,128)} %get-tuple-element.107, f32[8,8,8,64]{3,2,1,0:T(8,128)S(1)} %add_reduce_fusion.2, f32[8,8,64]{2,1,0:T(8,128)S(1)} %add.175), kind=kLoop, calls=%fused_computation.30 | loop fusion | flops 6258688 | bytes 8667136 | tf_op jit(solution)/shard_map/reduce_sum | solution.py:92
  502.1 33.0 %pmax.45 = f32[8192]{0:T(1024)S(1)} all-reduce(f32[8192]{0:T(1024)S(1)} %reshape.256), channel_id=1, replica_groups=mesh['item'=8,'code'=4] {'item'}, use_global_device_ids=true, to_apply=%region_26.27 | all-reduce | flops 8192 | bytes 65536 | tf_op jit(solution)/shard_map/pmax | solution.py:122
  535.1 33.2 %psum.61 = f32[8192]{0:T(1024)S(1)} all-reduce(f32[8192]{0:T(1024)S(1)} %exponential_multiply_fusion.1), channel_id=1, replica_groups=mesh['item'=8,'code'=4] {'item'}, use_global_device_ids=true, to_apply=%region_28.29 | all-reduce | flops 8192 | bytes 65536 | tf_op jit(solution)/shard_map/psum | solution.py:123
  569.5 7.6 %add_reduce_fusion.1 = f32[8,8,64]{2,1,0:T(8,128)S(1)} fusion(f32[8,8,8,64,64]{3,4,2,1,0:T(8,128)} %get-tuple-element.107, f32[8,8,8,64]{3,2,1,0:T(8,128)S(1)} %bitcast.99), kind=kLoop, calls=%fused_computation.35 | loop fusion | flops 4190208 | bytes 8536064 | tf_op jit(solution)/shard_map/reduce_max | solution.py:77
  577.1 7.6 %exponential_reduce_fusion.1 = f32[8,8,64]{2,1,0:T(8,128)S(1)} fusion(f32[8,8,8,64,64]{3,4,2,1,0:T(8,128)} %get-tuple-element.107, f32[8,8,64]{2,1,0:T(8,128)S(1)} %add_reduce_fusion.1, f32[8,8,8,64]{3,2,1,0:T(8,128)S(1)} %bitcast.100), kind=kLoop, calls=%fused_computation.29 | loop fusion | flops 6287360 | bytes 8552448 | tf_op jit(solution)/shard_map/reduce_sum | solution.py:78
  584.9 10.1 %pmax.46 = f32[4096]{0:T(1024)S(1)} all-reduce(f32[4096]{0:T(1024)S(1)} %reshape.261), channel_id=1, replica_groups=mesh['item'=8,'code'=4] {'code'}, use_global_device_ids=true, to_apply=%region_30.31 | all-reduce | flops 4096 | bytes 32768 | tf_op jit(solution)/shard_map/pmax | solution.py:84
  595.0 10.1 %psum.62 = f32[4096]{0:T(1024)S(1)} all-reduce(f32[4096]{0:T(1024)S(1)} %exponential_multiply_fusion.3), channel_id=1, replica_groups=mesh['item'=8,'code'=4] {'code'}, use_global_device_ids=true, to_apply=%region_32.33 | all-reduce | flops 4096 | bytes 32768 | tf_op jit(solution)/shard_map/psum | solution.py:85
  605.2 8.2 %add_reduce_fusion = f32[8,8,8,64]{3,2,1,0:T(8,128)S(1)} fusion(f32[8,8,8,64,64]{3,4,2,1,0:T(8,128)} %get-tuple-element.107, f32[8,8,64]{2,1,0:T(8,128)S(1)} %add.183), kind=kLoop, calls=%fused_computation.34 | loop fusion | flops 4161536 | bytes 8536064 | tf_op jit(solution)/shard_map/reduce_max | solution.py:91
  613.5 11.1 %exponential_reduce_fusion = f32[8,8,8,64]{3,2,1,0:T(8,128)S(1)} fusion(f32[8,8,8,64,64]{3,4,2,1,0:T(8,128)} %get-tuple-element.107, f32[8,8,8,64]{3,2,1,0:T(8,128)S(1)} %add_reduce_fusion, f32[8,8,64]{2,1,0:T(8,128)S(1)} %add.183), kind=kLoop, calls=%fused_computation.28 | loop fusion | flops 6258688 | bytes 8667136 | tf_op jit(solution)/shard_map/reduce_sum | solution.py:92
  633.1 33.0 %pmax.47 = f32[8192]{0:T(1024)S(1)} all-reduce(f32[8192]{0:T(1024)S(1)} %reshape.263), channel_id=1, replica_groups=mesh['item'=8,'code'=4] {'item'}, use_global_device_ids=true, to_apply=%region_37.38 | all-reduce | flops 8192 | bytes 65536 | tf_op jit(solution)/shard_map/pmax | solution.py:122
  666.1 33.0 %psum.63 = f32[8192]{0:T(1024)S(1)} all-reduce(f32[8192]{0:T(1024)S(1)} %exponential_multiply_fusion), channel_id=1, replica_groups=mesh['item'=8,'code'=4] {'item'}, use_global_device_ids=true, to_apply=%region_39.40 | all-reduce | flops 8192 | bytes 65536 | tf_op jit(solution)/shard_map/psum | solution.py:123
  (198 shorter events, 155.0 us)
Async XLA Ops:
  7.2 28.2 %copy-start = (s32[64,16]{0,1:T(8,128)S(1)}, s32[64,16]{0,1:T(8,128)}, u32[]{:S(2)}) copy-start(s32[64,16]{0,1:T(8,128)} %param.17) | copy-start | bytes 12292
  7.2 39.6 %all-gather.5.cloned.1.call-start = ((), (), s32[]{:S(2)}) async-start(), calls=%async_computation.1 | async-start | bytes 5242880 | tf_op jit(solution)/shard_map/all_gather | solution.py:17
  7.9 165.5 %all-gather.3.cloned.1.call-start = ((), (), s32[]{:S(2)}) async-start(), calls=%async_computation | async-start | bytes 9437184 | tf_op jit(solution)/shard_map/all_gather | solution.py:18
  35.4 4.6 copy-start.2
  302.9 10.7 %copy-start.1 = (f32[8,8,8,64,64]{3,4,2,1,0:T(8,128)S(1)}, f32[8,8,8,64,64]{3,4,2,1,0:T(8,128)}, u32[]{:S(2)}) copy-start(f32[8,8,8,64,64]{3,4,2,1,0:T(8,128)} %get-tuple-element.107) | copy-start | bytes 25165828
  302.9 37.6 %copy-start.3 = (f32[4096]{0:T(1024)S(1)}, f32[4096]{0:T(1024)}, u32[]{:S(2)}) copy-start(f32[4096]{0:T(1024)} %param.15) | copy-start | bytes 49156
  605.2 19.4 %copy-start.4 = (f32[4096]{0:T(1024)}, f32[4096]{0:T(1024)S(1)}, u32[]{:S(2)}) copy-start(f32[4096]{0:T(1024)S(1)} %add_subtract_fusion.3) | copy-start | bytes 49156
Sparse Core Ops, SparseCore 0:
  9.5 37.1 all-gather.4
  48.9 124.4 all-gather.2
where the time goes:
time: 708 us; the launch traced here: 707 us
  blocking collectives  286 us (40%)
  waiting for transfers between devices  127 us (18%)
  other arithmetic  127 us (18%)
  local copies, waits for them, and re-layouts  85.9 us (12%)
  matrix products  59.6 us (8%)
  between operations  15.8 us (2%)
    all_gather x1, waiting for transfers between devices, body(): code_cols = lax.all_gather(codebook, 'item', axis=0, tiled=True)  121 us
    pmax x3, blocking collectives, body(): joined_peak = lax.pmax(col_peak, 'item')  101 us
    psum x3, blocking collectives, body(): joined_total = lax.psum(col_total * jnp.exp(col_peak - joined_peak), 'item')  99.3 us
    dot_general x8, matrix products, build_tiles(): jnp.einsum('rbi,rbsj->bsij', own, picked, precision=lax.Precision.HIGHEST)  58.1 us
    gather x8, local copies, waits for them, and re-layouts, build_tiles(): picked = code_column_splits[:, ids, :]  49.4 us
    reduce_sum x3, other arithmetic, col_reduce(): block_total = jnp.sum(jnp.exp(logits - block_peak[:, :, None, :]), axis=2)  33.2 us
    psum x3, blocking collectives, body(): merged_total = lax.psum(row_total * jnp.exp(row_peak - merged_peak), 'code')  31.6 us
    pmax x3, blocking collectives, body(): merged_peak = lax.pmax(row_peak, 'code')  30.4 us
  transfers between devices with their start and end apart: 2, of which 2 were waited for; matrix products, arithmetic and copies ran while one was open for 2% of the time, Pallas kernels for 0%

commit v1 on v0

v1 whole, which is shorter than its diff:
```python
import functools
import math

import jax
import jax.numpy as jnp
from jax import lax
from jax.experimental import pallas as pl
from jax.experimental.pallas import tpu as pltpu
from jax.sharding import PartitionSpec as P

BLOCK = 64
LANES = 128
EXTRA = 8
ITERS = 3

masked_score = -1e30
softness_factor = 0.1

AXES = ("item", "code")


class Grid:
    def __init__(self, items, codes):
        self.items, self.codes = items, codes
        self.R, self.X = items // 2, codes // 2
        assert self.R & (self.R - 1) == 0 and self.X & (self.X - 1) == 0

    def perm(self, target):
        pairs = []
        for r in range(self.R):
            for y in range(2):
                for x in range(self.X):
                    for c in range(2):
                        to = target(r, y, x, c)
                        if to is not None:
                            pairs.append((self.index(r, y, x, c), self.index(*to)))
        return pairs

    def index(self, r, y, x, c):
        return (2 * r + y) * self.codes + 2 * x + c

    def send(self, value, target):
        return lax.ppermute(value, AXES, self.perm(target))


def low_half(shape):
    return lax.broadcasted_iota(jnp.int32, shape, len(shape) - 1) < BLOCK


def flip(v):
    return pltpu.roll(v, BLOCK, 1)


def prep_kernel(n_pos, scale, *refs):
    ins, out = refs[: 2 * n_pos], refs[2 * n_pos]
    columns = out.shape[1] * BLOCK
    for pos in range(n_pos):
        for g in range(columns // LANES):
            at = pl.ds(g * LANES, LANES)
            v = jnp.concatenate([ins[2 * pos][:, at], ins[2 * pos + 1][:, at]], axis=0) * scale
            high = v.astype(jnp.bfloat16).astype(jnp.float32)
            both = jnp.concatenate([high, v - high], axis=0).T.astype(jnp.bfloat16)
            both = jnp.concatenate([both, both], axis=1)
            per = LANES // BLOCK
            out[pos, pl.ds(g * per, per)] = both.reshape(per, BLOCK, both.shape[1])


def prep_items(chunks, scale, n_blocks):
    n_pos = len(chunks)
    half = chunks[0][0].shape[0]
    depth = 8 * half
    step = 8
    ins = [h for pair in chunks for h in pair]
    return pl.pallas_call(
        functools.partial(prep_kernel, n_pos, scale),
        grid=(n_blocks // step,),
        in_specs=[pl.BlockSpec((half, step * BLOCK), lambda i: (0, i))] * len(ins),
        out_specs=pl.BlockSpec((n_pos, step, BLOCK, depth), lambda i: (0, i, 0, 0)),
        out_shape=jax.ShapeDtypeStruct((n_pos, n_blocks, BLOCK, depth), jnp.bfloat16),
        name="prep_items",
    )(*ins)


def row_stats(logits, b, n_blocks, stats):
    peak = functools.reduce(jnp.maximum, logits)
    peak = jnp.max(peak, axis=1, keepdims=True)
    total = functools.reduce(jnp.add, [jnp.exp(v - peak) for v in logits])
    total = jnp.sum(total, axis=1, keepdims=True)
    lane = lax.broadcasted_iota(jnp.int32, stats.shape, 1)
    return jnp.where(lane == b, peak, jnp.where(lane == n_blocks + b, total, stats))


def score_kernel(n_cand, first, last, n_blocks, sel, qtab, *refs):
    refs = list(refs)
    own = [refs.pop(0) for _ in range(n_cand)]
    partner = [refs.pop(0) for _ in range(n_cand)]
    x_ref, base_ref = refs.pop(0), refs.pop(0)
    capacity_ref = refs.pop(0) if last else None
    tile_ref = refs.pop(0)
    stats_ref = refs.pop(0) if last else None
    stage, w_ref, sem = refs
    h = own[0].shape[0]
    groups = stage.shape[1] // LANES
    gb = x_ref.shape[1]
    slots = tile_ref.shape[2] // BLOCK
    step = pl.program_id(0)

    @pl.when(step == 0)
    def _():
        c = sel[2]
        for n in range(n_cand):

            @pl.when(sel[0] == n)
            def _():
                a = pltpu.make_async_copy(own[n], stage.at[pl.ds(pl.multiple_of(c * h, h), h)], sem.at[0])
                d = pltpu.make_async_copy(
                    partner[n], stage.at[pl.ds(pl.multiple_of((1 - c) * h, h), h)], sem.at[1]
                )
                a.start()
                d.start()
                a.wait()
                d.wait()

        def convert(g, carry):
            v = stage[:, pl.ds(pl.multiple_of(g * LANES, LANES), LANES)]
            for j, u in enumerate((v, flip(v))):
                high = u.astype(jnp.bfloat16)
                low = (u - high.astype(jnp.float32)).astype(jnp.bfloat16)
                w_ref[j * groups + g] = jnp.concatenate([high, low], axis=0)
            return carry

        lax.fori_loop(0, groups, convert, 0, unroll=2)
        if last:
            stats_ref[...] = jnp.zeros_like(stats_ref)
            stats_ref[pl.ds(BLOCK, EXTRA), :] = jnp.full(
                (EXTRA, stats_ref.shape[1]), jnp.sum(capacity_ref[...]), jnp.float32
            )

    rows = w_ref.shape[1]
    lower = lax.broadcasted_iota(jnp.int32, (rows, LANES), 1) < BLOCK

    def one(j, stats):
        b = step * gb + j
        parts = []
        for k in range(slots // 2):
            w = jnp.where(lower, w_ref[qtab[b * slots + 2 * k]], w_ref[qtab[b * slots + 2 * k + 1]])
            high, low = w[: rows // 2], w[rows // 2 :]
            parts.append(jnp.concatenate([high, high, low, low], axis=0))
        scores = jnp.dot(x_ref[0, j], jnp.concatenate(parts, axis=1), preferred_element_type=jnp.float32)
        base = base_ref[pl.ds(j, 1), :] if first else base_ref[j]
        scores = scores + base
        tile_ref[j] = scores
        if last:
            logits = [scores[:, k * LANES : (k + 1) * LANES] for k in range(slots // 2)]
            stats = row_stats(logits, b, n_blocks, stats)
        return stats

    if last:
        body = pl.ds(0, BLOCK)
        stats_ref[body, :] = lax.fori_loop(0, gb, one, stats_ref[body, :], unroll=2)
    else:
        lax.fori_loop(0, gb, one, 0, unroll=2)


def score_pass(sel, qtab, own, partner, x, base, capacity, n_blocks, slots, first, last):
    gb = 8
    h, codes = own[0].shape
    width = slots * BLOCK
    tile = jax.ShapeDtypeStruct((n_blocks, BLOCK, width), jnp.float32)
    tile_spec = pl.BlockSpec((gb, BLOCK, width), lambda i, *_: (i, 0, 0))
    base_spec = pl.BlockSpec((gb, width), lambda i, *_: (i, 0)) if first else tile_spec
    args = [*own, *partner, x, base]
    in_specs = [pl.BlockSpec(memory_space=pl.ANY)] * (2 * len(own)) + [
        pl.BlockSpec((1, gb, BLOCK, x.shape[3]), lambda i, sel, q: (sel[1], i, 0, 0)),
        base_spec,
    ]
    out_shape, out_specs = [tile], [tile_spec]
    if last:
        args.append(capacity)
        in_specs.append(pl.BlockSpec(capacity.shape, lambda i, *_: (0, 0)))
        shape = (BLOCK + EXTRA, 2 * n_blocks)
        out_shape.append(jax.ShapeDtypeStruct(shape, jnp.float32))
        out_specs.append(pl.BlockSpec(shape, lambda i, *_: (0, 0)))
    return pl.pallas_call(
        functools.partial(score_kernel, len(own), first, last, n_blocks),
        grid_spec=pltpu.PrefetchScalarGridSpec(
            num_scalar_prefetch=2,
            grid=(n_blocks // gb,),
            in_specs=in_specs,
            out_specs=out_specs,
            scratch_shapes=[
                pltpu.VMEM((2 * h, codes), jnp.float32),
                pltpu.VMEM((2 * codes // LANES, 4 * h, LANES), jnp.bfloat16),
                pltpu.SemaphoreType.DMA((2,)),
            ],
        ),
        out_shape=out_shape,
        input_output_aliases={} if first else {2 + 2 * len(own) + 1: 0},
        name="score",
    )(sel, qtab, *args)


def row_kernel(n_blocks, sel, ptab, own_ref, other_ref, tile_ref, stats_ref, g_ref):
    gb = tile_ref.shape[0]
    slots = tile_ref.shape[2] // BLOCK
    half = own_ref.shape[0]
    step = pl.program_id(0)

    @pl.when(step == 0)
    def _():
        c = sel[2]
        g_ref[pl.ds(pl.multiple_of(c * half, 8), half), :] = own_ref[...]
        g_ref[pl.ds(pl.multiple_of((1 - c) * half, 8), half), :] = other_ref[...]
        g_ref[pl.ds(2 * half, EXTRA), :] = jnp.zeros((EXTRA, LANES), jnp.float32)
        stats_ref[...] = jnp.zeros_like(stats_ref)

    lower = low_half((1, LANES))

    def one(j, stats):
        b = step * gb + j
        logits = []
        for k in range(slots // 2):
            p0, p1 = ptab[b * slots + 2 * k], ptab[b * slots + 2 * k + 1]
            g = jnp.where(lower, g_ref[pl.ds(p0, 1), :], g_ref[pl.ds(p1, 1), :])
            logits.append(tile_ref[j, :, k * LANES : (k + 1) * LANES] + g)
        return row_stats(logits, b, n_blocks, stats)

    stats_ref[...] = lax.fori_loop(0, gb, one, stats_ref[...], unroll=2)


def row_pass(sel, ptab, g_own, g_other, tiles):
    gb = 8
    n_blocks, _, width = tiles.shape
    shape = (BLOCK, 2 * n_blocks)
    whole = lambda a: pl.BlockSpec(a.shape, lambda i, *_: (0, 0))
    return pl.pallas_call(
        functools.partial(row_kernel, n_blocks),
        grid_spec=pltpu.PrefetchScalarGridSpec(
            num_scalar_prefetch=2,
            grid=(n_blocks // gb,),
            in_specs=[
                whole(g_own),
                whole(g_other),
                pl.BlockSpec((gb, BLOCK, width), lambda i, *_: (i, 0, 0)),
            ],
            out_specs=pl.BlockSpec(shape, lambda i, *_: (0, 0)),
            scratch_shapes=[pltpu.VMEM((2 * g_own.shape[0] + EXTRA, LANES), jnp.float32)],
        ),
        out_shape=jax.ShapeDtypeStruct(shape, jnp.float32),
        name="row_pass",
    )(sel, ptab, g_own, g_other, tiles)


def col_kernel(n_stats, n_blocks, start, sel, ptab, *refs):
    refs = list(refs)
    stat_refs = [refs.pop(0) for _ in range(n_stats)]
    weight_ref, norm_ref, tile_ref = refs.pop(0), refs.pop(0), refs.pop(0)
    keep_ref, send_ref, f_ref, cap_ref = (refs.pop(0) for _ in range(4))
    peak_ref, total_ref = refs.pop(0), refs.pop(0)
    slots = tile_ref.shape[2] // BLOCK
    maxes, sums = refs[:slots], refs[slots:]
    gb = tile_ref.shape[0]
    step = pl.program_id(0)

    @pl.when(step == 0)
    def _():
        rows = [r[pl.ds(0, BLOCK), :] for r in stat_refs]
        m = functools.reduce(jnp.maximum, rows)
        t = functools.reduce(
            jnp.add, [pltpu.roll(a, a.shape[1] - n_blocks, 1) * jnp.exp(a - m) for a in rows]
        )
        lane = lax.broadcasted_iota(jnp.int32, m.shape, 1)
        valid = lane < n_blocks
        t = jnp.where(valid, t, 1.0)
        f = jnp.log(weight_ref[...]) - (m + jnp.log(t))
        if not start:
            f = f - norm_ref[0:1, :]
        f_ref[...] = jnp.where(valid, f, 0.0)
        if start:
            caps = functools.reduce(jnp.add, [r[pl.ds(BLOCK, EXTRA), :] for r in stat_refs])
            cap_ref[...] = jnp.log(caps)
        else:
            cap_ref[...] = jnp.zeros_like(cap_ref)
        for s in range(slots):
            maxes[s][...] = jnp.full(maxes[s].shape, masked_score, jnp.float32)
            sums[s][...] = jnp.zeros(sums[s].shape, jnp.float32)

    f_all = f_ref[...]
    lane_f = lax.broadcasted_iota(jnp.int32, f_all.shape, 1)

    def one(j, carry):
        b = step * gb + j
        f = jnp.sum(jnp.where(lane_f == b, f_all, 0.0), axis=1, keepdims=True)
        for k in range(slots // 2):
            at = slice(k * LANES, (k + 1) * LANES)
            logits = tile_ref[j, :, at] + f
            peak = jnp.max(logits, axis=0, keepdims=True)
            total = jnp.sum(jnp.exp(logits - peak), axis=0, keepdims=True)
            peak_ref[k, pl.ds(b, 1), :] = peak
            total_ref[k, pl.ds(b, 1), :] = total
            for s in (2 * k, 2 * k + 1):
                row = pl.ds(ptab[b * slots + s], 1)
                maxes[s][row, :] = jnp.maximum(maxes[s][row, :], peak)
        return carry

    lax.fori_loop(0, gb, one, 0, unroll=2)

    @pl.when(step == pl.num_programs(0) - 1)
    def _():
        lower = low_half(maxes[0].shape)

        def joined(parts, op):
            even = functools.reduce(op, [parts[s][...] for s in range(0, slots, 2)])
            odd = functools.reduce(op, [parts[s][...] for s in range(1, slots, 2)])
            return jnp.where(lower, op(even, flip(odd)), op(odd, flip(even)))

        top = joined(maxes, jnp.maximum)
        maxes[0][...] = top
        lower_row = low_half((1, LANES))

        def spread(b, carry):
            for k in range(slots // 2):
                p0, p1 = ptab[b * slots + 2 * k], ptab[b * slots + 2 * k + 1]
                peak = jnp.where(lower_row, maxes[0][pl.ds(p0, 1), :], maxes[0][pl.ds(p1, 1), :])
                part = total_ref[k, pl.ds(b, 1), :] * jnp.exp(peak_ref[k, pl.ds(b, 1), :] - peak)
                for s, p in ((2 * k, p0), (2 * k + 1, p1)):
                    sums[s][pl.ds(p, 1), :] += part
            return carry

        lax.fori_loop(0, n_blocks, spread, 0, unroll=4)
        maxes[1][...] = jnp.where(lower, top, joined(sums, jnp.add))
        c = sel[2]
        half = keep_ref.shape[0] - EXTRA
        body, tail = pl.ds(0, half), pl.ds(half, EXTRA)
        keep_ref[body, :] = maxes[1][pl.ds(pl.multiple_of(c * half, 8), half), :]
        send_ref[body, :] = maxes[1][pl.ds(pl.multiple_of((1 - c) * half, 8), half), :]
        weights = jnp.where(lane_f < n_blocks, weight_ref[...], 0.0)
        weights = jnp.full((EXTRA, LANES), jnp.sum(weights), jnp.float32)
        keep_ref[tail, :] = weights
        send_ref[tail, :] = weights


def col_pass(sel, ptab, stats, weights, norm, tiles, code_blocks, start):
    gb = 8
    n_blocks, _, width = tiles.shape
    slots = width // BLOCK
    whole = lambda a: pl.BlockSpec(a.shape, lambda i, *_: (0, 0))
    half = jax.ShapeDtypeStruct((code_blocks // 2 + EXTRA, LANES), jnp.float32)
    outs = [
        half,
        half,
        jax.ShapeDtypeStruct(weights.shape, jnp.float32),
        jax.ShapeDtypeStruct((EXTRA, stats[0].shape[1]), jnp.float32),
    ]
    return pl.pallas_call(
        functools.partial(col_kernel, len(stats), n_blocks, start),
        grid_spec=pltpu.PrefetchScalarGridSpec(
            num_scalar_prefetch=2,
            grid=(n_blocks // gb,),
            in_specs=[whole(a) for a in (*stats, weights, norm)]
            + [pl.BlockSpec((gb, BLOCK, width), lambda i, *_: (i, 0, 0))],
            out_specs=[whole(a) for a in outs],
            scratch_shapes=[pltpu.VMEM((slots // 2, n_blocks, LANES), jnp.float32)] * 2
            + [pltpu.VMEM((code_blocks + EXTRA, LANES), jnp.float32)] * (2 * slots),
        ),
        out_shape=outs,
        name="col_pass",
    )(sel, ptab, *stats, weights, norm, tiles)


def merge(parts):
    lower = low_half(parts[0].shape)
    flips = [flip(a) for a in parts]
    peaks = [jnp.where(lower, a, b) for a, b in zip(parts, flips)]
    totals = [jnp.where(lower, b, a) for a, b in zip(parts, flips)]
    peak = functools.reduce(jnp.maximum, peaks)
    total = functools.reduce(jnp.add, [t * jnp.exp(p - peak) for p, t in zip(peaks, totals)])
    return peak, total


def join_kernel(a_ref, b_ref, out_ref):
    half = out_ref.shape[0] - EXTRA
    body, tail = pl.ds(0, half), pl.ds(half, EXTRA)
    peak, total = merge([a_ref[body, :], b_ref[body, :]])
    out_ref[body, :] = jnp.where(low_half(peak.shape), peak, total)
    out_ref[tail, :] = a_ref[tail, :] + b_ref[tail, :]


def join(a, b):
    return pl.pallas_call(join_kernel, out_shape=jax.ShapeDtypeStruct(a.shape, jnp.float32), name="join")(a, b)


def finish_kernel(n, start, sel, *refs):
    parts = refs[:n]
    capacity_ref, cap_ref, g_ref, norm_ref = refs[n:]
    half = g_ref.shape[0]
    body, tail = pl.ds(0, half), pl.ds(half, EXTRA)
    peak, total = merge([r[body, :] for r in parts])
    capacity = capacity_ref[pl.ds(pl.multiple_of(sel[2] * half, 8), half), :]
    g = jnp.log(capacity) - cap_ref[0:1, 0:LANES] - (peak + jnp.log(total))
    norm = jnp.log(functools.reduce(jnp.add, [r[tail, :] for r in parts]))
    norm_ref[...] = norm
    g_ref[...] = g + norm[0:1, :] if start else g


def finish(sel, parts, capacity, cap, start):
    half = capacity.shape[0] // 2
    whole = pl.BlockSpec(memory_space=pltpu.VMEM)
    return pl.pallas_call(
        functools.partial(finish_kernel, len(parts), start),
        in_specs=[pl.BlockSpec(memory_space=pltpu.SMEM)] + [whole] * (len(parts) + 2),
        out_specs=[whole, whole],
        out_shape=[
            jax.ShapeDtypeStruct((half, LANES), jnp.float32),
            jax.ShapeDtypeStruct((EXTRA, LANES), jnp.float32),
        ],
        name="finish",
    )(sel, *parts, capacity, cap)


def compact(pairs, slots, code_blocks):
    live = pairs >= 0
    rank = jnp.cumsum(live.astype(jnp.int32), axis=1) - 1
    hit = live[:, :, None] & (rank[:, :, None] == jnp.arange(slots, dtype=jnp.int32))
    return code_blocks + jnp.sum(jnp.where(hit, pairs[:, :, None] - code_blocks, 0), axis=1)


def body(grid, residuals, codebook, item_weight, code_capacity, pairs):
    R, X = grid.R, grid.X
    r, y = lax.axis_index("item") // 2, lax.axis_index("item") % 2
    x, c = lax.axis_index("code") // 2, lax.axis_index("code") % 2
    width = residuals.shape[0] * grid.codes
    n_items, n_codes = residuals.shape[1], codebook.shape[1]
    n_blocks, code_blocks = n_items // BLOCK, n_codes // BLOCK
    slots = pairs.shape[1] // 2
    scale = 1.0 / (softness_factor * math.sqrt(width))
    swapped = lambda r, y, x, c: (r, c, x, y)
    to_core = lambda r, y, x, c: (r, y, x, 1 - c)
    to_y = lambda r, y, x, c: (r, 1 - y, x, c)

    codes = grid.send(codebook, swapped)
    small = jnp.concatenate(
        [
            pairs.astype(jnp.float32).reshape(-1),
            item_weight,
            code_capacity,
        ]
    ).reshape(-1, LANES)
    small = grid.send(small, swapped).reshape(-1)
    n_pairs = pairs.size
    pairs = small[:n_pairs].reshape(pairs.shape).astype(jnp.int32)
    weights = small[n_pairs : n_pairs + n_items].reshape(n_blocks, BLOCK).T
    weights = jnp.concatenate([weights, jnp.ones_like(weights)], axis=1)
    capacity = small[n_pairs + n_items :].reshape(code_blocks, BLOCK)
    capacity_sum = capacity.reshape(-1, LANES)
    capacity = jnp.concatenate([capacity, capacity], axis=1)

    residuals, codes = lax.optimization_barrier((residuals, codes))
    ups, downs = {0: codes}, {0: codes}
    for s in range(1, R):
        ups[s] = grid.send(ups[s - 1], lambda r, y, x, c: (r + 1, y, x, c) if s - 1 <= r < R - 1 else None)
        downs[s] = grid.send(downs[s - 1], lambda r, y, x, c: (r - 1, y, x, c) if 0 < r <= R - s else None)
    up_partner = {0: grid.send(codes, to_core)}
    down_partner = {0: up_partner[0]}
    for s in range(1, R):
        up_partner[s] = grid.send(ups[s], lambda r, y, x, c: (r, y, x, 1 - c) if r >= s else None)
        down_partner[s] = grid.send(downs[s], lambda r, y, x, c: (r, y, x, 1 - c) if r < R - s else None)

    items = grid.send(residuals, swapped)
    halves = lambda v: (v[: v.shape[0] // 2], v[v.shape[0] // 2 :])
    from_y = grid.send(items, to_y)
    chunks = [halves(items), halves(from_y)]
    for m in range(1, X):
        to_x = lambda r, y, x, c: (r, y, x ^ m, c)
        from_x = grid.send(items, to_x)
        chunks.append(halves(from_x))
        chunks.append((grid.send(chunks[1][0], to_x), grid.send(halves(from_x)[1], to_y)))
    x_all = prep_items(chunks, scale, n_blocks)

    ids = compact(pairs, slots, code_blocks)
    live = ids < code_blocks
    ptab = ids.reshape(-1)
    safe = jnp.where(live, ids, 0)
    parity = (safe + jnp.arange(slots, dtype=jnp.int32)) % 2
    qtab = (parity * (code_blocks // 2) + safe // 2).reshape(-1)
    penalty = jnp.repeat(jnp.where(live, 0.0, masked_score).astype(jnp.float32), BLOCK, axis=1)

    order = []
    for me in range(R):
        arrivals = [(s, side, me - s if side == 0 else me + s) for s in range(1, R) for side in (0, 1)]
        order.append([(0, 0, me)] + [a for a in arrivals if 0 <= a[2] < R])
    tiles, stats = penalty, None
    for n in range(R):
        cands = sorted({o[n][:2] for o in order})
        pick = jnp.array([cands.index(o[n][:2]) for o in order], jnp.int32)[r]
        source = jnp.array([o[n][2] for o in order], jnp.int32)[r]
        sel = jnp.stack([pick, source ^ (2 * x + y), c, c]).astype(jnp.int32)
        own = [(ups, downs)[side][s] for s, side in cands]
        partner = [(up_partner, down_partner)[side][s] for s, side in cands]
        out = score_pass(
            sel, qtab, own, partner, x_all, tiles, capacity_sum, n_blocks, slots, n == 0, n == R - 1
        )
        tiles = out[0]
    stats = out[1]

    norm = jnp.zeros((EXTRA, LANES), jnp.float32)
    cap = None
    for sweep in range(ITERS):
        start = sweep == 0
        parts = [stats]
        for m in range(1, 2 * X):
            parts.append(grid.send(stats, lambda r, y, x, c: (r, y ^ (m & 1), x ^ (m >> 1), c)))
        keep, give, f, new_cap = col_pass(sel, ptab, parts, weights, norm, tiles, code_blocks, start)
        cap = new_cap if start else cap
        mine = join(keep, grid.send(give, to_core))
        parts = [mine]
        for m in range(1, R):
            parts.append(grid.send(mine, lambda r, y, x, c: (r ^ m, y, x, c)))
        g, new_norm = finish(sel, parts, capacity, cap, start)
        norm = new_norm if start else norm
        if sweep < ITERS - 1:
            stats = row_pass(sel, ptab, g, grid.send(g, to_core), tiles)

    item_potential = grid.send(f[:, :n_blocks].T.reshape(n_items), swapped)
    g = g[:, :BLOCK]
    near = grid.send(g, swapped)
    far = grid.send(g, lambda r, y, x, c: (r, 1 - c, x, y))
    code_potential = jnp.where(y == 0, jnp.concatenate([near, far]), jnp.concatenate([far, near]))
    return item_potential, code_potential.reshape(n_codes)


def solution(mesh):
    placed = (P("code", "item"), P("item", "code"), P("item"), P("code"), P("item", "code"))
    grid = Grid(mesh.shape["item"], mesh.shape["code"])
    return jax.shard_map(
        functools.partial(body, grid),
        mesh=mesh,
        in_specs=placed,
        out_specs=(P("item"), P("code")),
        check_vma=False,
    )
```

time: 708 us -> 327 us (0.46)
  blocking collectives: 286 us -> 0 us
  Pallas kernels: 0 us -> 143 us
  other arithmetic: 127 us -> 7.5 us
  starting transfers between devices: 0.08 us -> 82.4 us
  waiting for transfers between devices: 127 us -> 60.2 us
  matrix products: 59.6 us -> 0 us
  local copies, waits for them, and re-layouts: 85.9 us -> 26.6 us
  between operations: 15.8 us -> 3.05 us
    psum x7 -> x0, blocking collectives: 155 us -> none  [the longest x3 99.3 us: body(): joined_total = lax.psum(col_total * jnp.exp(col_peak - joined_peak), 'item')]
    pallas_call x0 -> x16, Pallas kernels: none -> 143 us  [the longest x4 70.4 us: score_pass(): pl.pallas_call(functools.partial(score_kernel, len(own), first, last, n_b...]
    pmax x6 -> x0, blocking collectives: 132 us -> none  [the longest x3 101 us: body(): joined_peak = lax.pmax(col_peak, 'item')]
    all_gather x2 -> x0, waiting for transfers between devices: 125 us -> none  [the longest x1 121 us: body(): code_cols = lax.all_gather(codebook, 'item', axis=0, tiled=True)]
    ppermute x0 -> x46, starting transfers between devices: none -> 82.4 us  [send(): return lax.ppermute(value, AXES, self.perm(target))]
    reduce_max x12 -> x0, other arithmetic: 68.7 us -> none  [the longest x3 24.6 us: col_reduce(): block_peak = jnp.max(logits, axis=2)]
    ppermute x0 -> x46, waiting for transfers between devices: none -> 60.2 us  [send(): return lax.ppermute(value, AXES, self.perm(target))]
    gather x19 -> x0, local copies, waits for them, and re-layouts: 59.8 us -> none  [the longest x8 49.4 us: build_tiles(): picked = code_column_splits[:, ids, :]]
  transfers between devices with their start and end apart: 2 -> 46, of which waited for: 2 -> 27; matrix products, arithmetic and copies ran while one was open for 2% -> 8% of each run, Pallas kernels for 0% -> 19%
where the time goes in v1:
time: 327 us; the launch traced here: 322 us
  Pallas kernels  143 us (44%)
  starting transfers between devices  82.4 us (25%)
  waiting for transfers between devices  60.2 us (18%)
  local copies, waits for them, and re-layouts  26.6 us (8%)
  other arithmetic  7.5 us (2%)
    ppermute x46, starting transfers between devices, send(): return lax.ppermute(value, AXES, self.perm(target))  82.4 us
    pallas_call x4, Pallas kernels, score_pass(): pl.pallas_call(functools.partial(score_kernel, len(own), first, last, n_b...  70.4 us
    ppermute x46, waiting for transfers between devices, send(): return lax.ppermute(value, AXES, self.perm(target))  60.2 us
    pallas_call x3, Pallas kernels, col_pass(): pl.pallas_call(functools.partial(col_kernel, len(stats), n_blocks, start)...  33 us
    pallas_call x2, Pallas kernels, row_pass(): pl.pallas_call(functools.partial(row_kernel, n_blocks), grid_spec=pltpu.P...  21.4 us
    pallas_call x1, Pallas kernels, prep_items(): pl.pallas_call(functools.partial(prep_kernel, n_pos, scale), grid=(n_bloc...  8.28 us
    slice x3, local copies, waits for them, and re-layouts, body(): halves = lambda v: (v[:v.shape[0] // 2], v[v.shape[0] // 2:])  6.81 us
    unnamed x59, local copies, waits for them, and re-layouts  6.73 us
  transfers between devices with their start and end apart: 46, of which 27 were waited for; matrix products, arithmetic and copies ran while one was open for 8% of the time, Pallas kernels for 19%

profile of v1, /device:TPU:0, one launch (start us, length us, event | category | flops | bytes accessed | tf_op | source)
XLA Modules:
  0.0 322.4 jit_solution(17289561413357101673)
XLA Ops:
  2.5 9.4 %collective-permute-start.12 = (f32[64,4096]{1,0:T(8,128)}, f32[64,4096]{1,0:T(8,128)}, u32[]{:S(2)}, u32[]{:S(2)}) collective-permute-start(f32[64,4096]{1,0:T(8,128)} %param.13), channel_id=1, source_target_pairs={{0,0},{1,4},{2,2},{3,6},{4,1},{5,5},{6,3},{7,7},{8,8},{9,12},{10,1... | collective-permute-start | bytes 3145736 | tf_op jit(solution)/shard_map/ppermute | solution.py:43
  13.2 6.6 %collective-permute-start.2 = (f32[32,8192]{1,0:T(8,128)S(1)}, f32[32,8192]{1,0:T(8,128)}, u32[]{:S(2)}, u32[]{:S(2)}) collective-permute-start(f32[32,8192]{1,0:T(8,128)S(1)} %collective-permute-done.1.refs_0_), channel_id=1, source_target_pairs={{0,8},{1,9},{2,10},{3,11},{4,12},{5,13},{6,14},{7,15},{8,16},{9,17... | collective-permute-start | bytes 3145736 | tf_op jit(solution)/shard_map/ppermute | solution.py:43
  22.2 14.2 %collective-permute-start.13 = (f32[64,4096]{1,0:T(8,128)}, f32[64,4096]{1,0:T(8,128)}, u32[]{:S(2)}, u32[]{:S(2)}) collective-permute-start(f32[64,4096]{1,0:T(8,128)} %collective-permute-done.12), channel_id=1, source_target_pairs={{0,4},{1,5},{2,6},{3,7},{4,0},{5,1},{6,2},{7,3},{8,12},{9,13},{10,... | collective-permute-start | bytes 3145736 | tf_op jit(solution)/shard_map/ppermute | solution.py:43
  54.8 5.7 %collective-permute-done.13 = f32[64,4096]{1,0:T(8,128)} collective-permute-done((f32[64,4096]{1,0:T(8,128)}, f32[64,4096]{1,0:T(8,128)}, u32[]{:S(2)}, u32[]{:S(2)}) %collective-permute-start.13) | collective-permute-done | bytes 1048608 | tf_op jit(solution)/shard_map/ppermute | solution.py:43
  60.4 1.9 collective-permute-start.17
  62.4 2.2 fusion.9
  64.6 10.4 %collective-permute-done.14 = f32[64,4096]{1,0:T(8,128)} collective-permute-done((f32[64,4096]{1,0:T(8,128)}, f32[64,4096]{1,0:T(8,128)}, u32[]{:S(2)}, u32[]{:S(2)}) %collective-permute-start.14) | collective-permute-done | bytes 1048608 | tf_op jit(solution)/shard_map/ppermute | solution.py:43
  80.6 2.2 fusion.8
  86.9 1.9 collective-permute-start.9
  88.8 7.2 %collective-permute-done.16.refs_7_ = f32[32,4096]{1,0:T(8,128)} collective-permute-done((f32[32,4096]{1,0:T(8,128)}, f32[32,4096]{1,0:T(8,128)}, u32[]{:S(2)}, u32[]{:S(2)}) %collective-permute-start.16) | collective-permute-done | bytes 524320 | tf_op jit(solution)/shard_map/ppermute | solution.py:43
  97.7 4.4 %collective-permute-done.7.refs_3_ = f32[32,8192]{1,0:T(8,128)} collective-permute-done((f32[32,8192]{1,0:T(8,128)S(1)}, f32[32,8192]{1,0:T(8,128)}, u32[]{:S(2)}, u32[]{:S(2)}) %collective-permute-start.7) | collective-permute-done | bytes 1048608 | tf_op jit(solution)/shard_map/ppermute | solution.py:43
  102.1 1.9 collective-permute-start.11
  107.9 2.3 fusion.10
  110.2 8.3 %prep_items.1.refs_2_.refs_4_.refs_6_.refs_8_ = bf16[4,64,64,256]{3,2,1,0:T(8,128)(2,1)} custom-call(f32[32,4096]{1,0:T(8,128)} %get-tuple-element.39.refs_0_, f32[32,4096]{1,0:T(8,128)} %get-tuple-element.38.refs_1_, f32[32,4096]{1,0:T(8,128)} %get-tuple-element.37.refs_2_, f32[32,4096]{1,0:T(8,128)} %get-tuple-element.36.refs_3_, ...), custom_call_target="tpu_custom_call" | custom-call | tf_op jit(solution)/shard_map/prep_items/pallas_call | solution.py:74
  118.5 15.0 %score.4.refs_5_ = f32[64,64,512]{2,1,0:T(8,128)} custom-call(s32[4]{0:T(128)} %add_add_fusion.3.sel, s32[512]{0:T(512)} %fusion.5.qtab, f32[32,8192]{1,0:T(8,128)} %copy-done.3, f32[32,8192]{1,0:T(8,128)} %collective-permute-done.19.refs_1_, bf16[4,64,64,256]{3,2,1,0:T(8,128)(2,1)} %prep_items.1.refs_2_.refs_4_.refs_6_.refs_8_, f32[64,512]{1,0:T(8,128)} %reshape.74.refs_3_), custom_call_target="tpu_custom_call" | custom-call | tf_op jit(solution)/shard_map/score/pallas_call | solution.py:184
  133.6 17.4 %score.5.refs_7_ = f32[64,64,512]{2,1,0:T(8,128)} custom-call(s32[4]{0:T(128)} %add_add_fusion.2.sel, s32[512]{0:T(512)} %fusion.5.qtab, f32[32,8192]{1,0:T(8,128)} %collective-permute-done.2.refs_0_, f32[32,8192]{1,0:T(8,128)} %copy-done, f32[32,8192]{1,0:T(8,128)} %collective-permute-done.18.refs_2_, ...), custom_call_target="tpu_custom_call", output_to_operand_aliasing={{}: (7, {})} | custom-call | tf_op jit(solution)/shard_map/score/pallas_call | solution.py:184
  151.0 17.4 %score.6.refs_9_ = f32[64,64,512]{2,1,0:T(8,128)} custom-call(s32[4]{0:T(128)} %add_add_fusion.1.sel, s32[512]{0:T(512)} %fusion.5.qtab, f32[32,8192]{1,0:T(8,128)} %copy-done, f32[32,8192]{1,0:T(8,128)} %copy-done.2, f32[32,8192]{1,0:T(8,128)} %copy-done.1, f32[32,8192]{1,0:T(8,128)} %collective-permute-done.17.refs_3_, ...), custom_call_target="tpu_custom_call", output_to_operand_aliasing={{}: (9, {})} | custom-call | tf_op jit(solution)/shard_map/score/pallas_call | solution.py:184
  168.5 20.5 %score.7 = (f32[64,64,512]{2,1,0:T(8,128)}, f32[72,128]{1,0:T(8,128)}) custom-call(s32[4]{0:T(128)} %add_add_fusion.sel, s32[512]{0:T(512)} %fusion.5.qtab, f32[32,8192]{1,0:T(8,128)} %copy-done.2, f32[32,8192]{1,0:T(8,128)} %copy-done.1, f32[32,8192]{1,0:T(8,128)} %collective-permute-done.6.refs_2_, ...), custom_call_target="tpu_custom_call", output_to_operand_aliasing={{0}: (11, {})} | custom-call | tf_op jit(solution)/shard_map/score/pallas_call | solution.py:184
  189.0 3.4 %collective-permute-start.20 = (f32[72,128]{1,0:T(8,128)}, f32[72,128]{1,0:T(8,128)S(1)}, u32[]{:S(2)}, u32[]{:S(2)}) collective-permute-start(f32[72,128]{1,0:T(8,128)} %get-tuple-element.20.refs_0_), channel_id=1, source_target_pairs={{0,4},{1,5},{2,6},{3,7},{4,0},{5,1},{6,2},{7,3},{8,12},{9,13},{10,... | collective-permute-start | bytes 110600 | tf_op jit(solution)/shard_map/ppermute | solution.py:43
  199.0 11.0 %col_pass.3 = (f32[72,128]{1,0:T(8,128)}, f32[72,128]{1,0:T(8,128)}, f32[64,128]{1,0:T(8,128)}, f32[8,128]{1,0:T(8,128)}) custom-call(s32[4]{0:T(128)} %add_add_fusion.sel, s32[512]{0:T(512)} %copy-done.5, f32[72,128]{1,0:T(8,128)} %get-tuple-element.20.refs_0_, f32[72,128]{1,0:T(8,128)} %copy-done.6, f32[72,128]{1,0:T(8,128)} %copy-done.7, ...), custom_call_target="tpu_custom_call" | custom-call | tf_op jit(solution)/shard_map/col_pass/pallas_call | solution.py:355
  213.6 3.6 %collective-permute-start.25 = (f32[72,128]{1,0:T(8,128)}, f32[72,128]{1,0:T(8,128)S(1)}, u32[]{:S(2)}, u32[]{:S(2)}) collective-permute-start(f32[72,128]{1,0:T(8,128)} %join.3.refs_0_), channel_id=1, source_target_pairs={{0,16},{1,17},{2,18},{3,19},{4,20},{5,21},{6,22},{7,23},{8,24},{9,... | collective-permute-start | bytes 110600 | tf_op jit(solution)/shard_map/ppermute | solution.py:43
  219.7 3.3 %collective-permute-done.26.refs_3_ = f32[72,128]{1,0:T(8,128)S(1)} collective-permute-done((f32[72,128]{1,0:T(8,128)}, f32[72,128]{1,0:T(8,128)S(1)}, u32[]{:S(2)}, u32[]{:S(2)}) %collective-permute-start.26) | collective-permute-done | bytes 36896 | tf_op jit(solution)/shard_map/ppermute | solution.py:43
  227.4 10.7 %row_pass.2.refs_0_ = f32[64,128]{1,0:T(8,128)} custom-call(s32[4]{0:T(128)} %add_add_fusion.sel, s32[512]{0:T(512)} %copy-done.5, f32[64,128]{1,0:T(8,128)} %get-tuple-element.25.own_ref, f32[64,128]{1,0:T(8,128)} %copy-done.27, f32[64,64,512]{2,1,0:T(8,128)} %get-tuple-element.21.refs_6_.tile_ref), custom_call_target="tpu_custom_call" | custom-call | tf_op jit(solution)/shard_map/row_pass/pallas_call | solution.py:236
  239.7 1.9 collective-permute-start.30
  242.7 2.0 collective-permute-done.30.refs_3_
  245.3 11.0 %col_pass.4 = (f32[72,128]{1,0:T(8,128)}, f32[72,128]{1,0:T(8,128)}, f32[64,128]{1,0:T(8,128)}, f32[8,128]{1,0:T(8,128)}) custom-call(s32[4]{0:T(128)} %add_add_fusion.sel, s32[512]{0:T(512)} %copy-done.5, f32[64,128]{1,0:T(8,128)} %row_pass.2.refs_0_, f32[64,128]{1,0:T(8,128)} %copy-done.22, f32[64,128]{1,0:T(8,128)} %copy-done.24, f32[64,128]{1,0:T(8,128)} %copy-done.26, ...), custom_call_target="tpu_custom_call" | custom-call | tf_op jit(solution)/shard_map/col_pass/pallas_call | solution.py:355
  261.0 3.3 %collective-permute-start.34 = (f32[72,128]{1,0:T(8,128)}, f32[72,128]{1,0:T(8,128)S(1)}, u32[]{:S(2)}, u32[]{:S(2)}) collective-permute-start(f32[72,128]{1,0:T(8,128)} %join.4.refs_0_), channel_id=1, source_target_pairs={{0,24},{1,25},{2,26},{3,27},{4,28},{5,29},{6,30},{7,31},{8,16},{9,... | collective-permute-start | bytes 110600 | tf_op jit(solution)/shard_map/ppermute | solution.py:43
  264.9 2.0 collective-permute-done.34.refs_3_
  271.2 10.7 %row_pass.3.refs_0_ = f32[64,128]{1,0:T(8,128)} custom-call(s32[4]{0:T(128)} %add_add_fusion.sel, s32[512]{0:T(512)} %copy-done.5, f32[64,128]{1,0:T(8,128)} %get-tuple-element.29.own_ref, f32[64,128]{1,0:T(8,128)} %copy-done.28, f32[64,64,512]{2,1,0:T(8,128)} %get-tuple-element.21.refs_6_.tile_ref), custom_call_target="tpu_custom_call" | custom-call | tf_op jit(solution)/shard_map/row_pass/pallas_call | solution.py:236
  290.4 11.0 %col_pass.5 = (f32[72,128]{1,0:T(8,128)}, f32[72,128]{1,0:T(8,128)}, f32[64,128]{1,0:T(8,128)}, f32[8,128]{1,0:T(8,128)}) custom-call(s32[4]{0:T(128)} %add_add_fusion.sel, s32[512]{0:T(512)} %copy-done.5, f32[64,128]{1,0:T(8,128)} %row_pass.3.refs_0_, f32[64,128]{1,0:T(8,128)} %copy-done.21, f32[64,128]{1,0:T(8,128)} %copy-done.23, f32[64,128]{1,0:T(8,128)} %copy-done.25, ...), custom_call_target="tpu_custom_call" | custom-call | tf_op jit(solution)/shard_map/col_pass/pallas_call | solution.py:355
  305.3 3.2 collective-permute-start.42
  311.1 3.3 %collective-permute-done.43.refs_3_ = f32[72,128]{1,0:T(8,128)S(1)} collective-permute-done((f32[72,128]{1,0:T(8,128)}, f32[72,128]{1,0:T(8,128)S(1)}, u32[]{:S(2)}, u32[]{:S(2)}) %collective-permute-start.43) | collective-permute-done | bytes 36896 | tf_op jit(solution)/shard_map/ppermute | solution.py:43
  (186 shorter events, 89.6 us)
Async XLA Ops:
  2.5 19.6 %collective-permute-start.12 = (f32[64,4096]{1,0:T(8,128)}, f32[64,4096]{1,0:T(8,128)}, u32[]{:S(2)}, u32[]{:S(2)}) collective-permute-start(f32[64,4096]{1,0:T(8,128)} %param.13), channel_id=1, source_target_pairs={{0,0},{1,4},{2,2},{3,6},{4,1},{5,5},{6,3},{7,7},{8,8},{9,12},{10,1... | collective-permute-start | bytes 3145736 | tf_op jit(solution)/shard_map/ppermute | solution.py:43
  11.9 40.4 %collective-permute-start.4 = (f32[32,8192]{1,0:T(8,128)S(1)}, f32[32,8192]{1,0:T(8,128)S(1)}, u32[]{:S(2)}, u32[]{:S(2)}) collective-permute-start(f32[32,8192]{1,0:T(8,128)S(1)} %collective-permute-done.1.refs_0_), channel_id=1, source_target_pairs={{8,0},{9,1},{10,2},{11,3},{12,4},{13,5},{14,6},{15,7},{16,8},{17,9... | collective-permute-start | bytes 3145736 | tf_op jit(solution)/shard_map/ppermute | solution.py:43
  13.2 40.5 %collective-permute-start.2 = (f32[32,8192]{1,0:T(8,128)S(1)}, f32[32,8192]{1,0:T(8,128)}, u32[]{:S(2)}, u32[]{:S(2)}) collective-permute-start(f32[32,8192]{1,0:T(8,128)S(1)} %collective-permute-done.1.refs_0_), channel_id=1, source_target_pairs={{0,8},{1,9},{2,10},{3,11},{4,12},{5,13},{6,14},{7,15},{8,16},{9,17... | collective-permute-start | bytes 3145736 | tf_op jit(solution)/shard_map/ppermute | solution.py:43
  21.5 29.1 %collective-permute-start = (f32[104,128]{1,0:T(8,128)S(1)}, f32[104,128]{1,0:T(8,128)S(1)}, u32[]{:S(2)}, u32[]{:S(2)}) collective-permute-start(f32[104,128]{1,0:T(8,128)S(1)} %maximum_bitcast_fusion), channel_id=1, source_target_pairs={{0,0},{1,4},{2,2},{3,6},{4,1},{5,5},{6,3},{7,7},{8,8},{9,12},{10,1... | collective-permute-start | bytes 159752 | tf_op jit(solution)/shard_map/ppermute | solution.py:43
  22.2 38.3 %collective-permute-start.13 = (f32[64,4096]{1,0:T(8,128)}, f32[64,4096]{1,0:T(8,128)}, u32[]{:S(2)}, u32[]{:S(2)}) collective-permute-start(f32[64,4096]{1,0:T(8,128)} %collective-permute-done.12), channel_id=1, source_target_pairs={{0,4},{1,5},{2,6},{3,7},{4,0},{5,1},{6,2},{7,3},{8,12},{9,13},{10,... | collective-permute-start | bytes 3145736 | tf_op jit(solution)/shard_map/ppermute | solution.py:43
  50.8 24.1 %collective-permute-start.14 = (f32[64,4096]{1,0:T(8,128)}, f32[64,4096]{1,0:T(8,128)}, u32[]{:S(2)}, u32[]{:S(2)}) collective-permute-start(f32[64,4096]{1,0:T(8,128)} %collective-permute-done.12), channel_id=1, source_target_pairs={{0,2},{1,3},{2,0},{3,1},{4,6},{5,7},{6,4},{7,5},{8,10},{9,11},{10,... | collective-permute-start | bytes 3145736 | tf_op jit(solution)/shard_map/ppermute | solution.py:43
  52.4 25.2 %collective-permute-start.5 = (f32[32,8192]{1,0:T(8,128)S(1)}, f32[32,8192]{1,0:T(8,128)S(1)}, u32[]{:S(2)}, u32[]{:S(2)}) collective-permute-start(f32[32,8192]{1,0:T(8,128)S(1)} %collective-permute-done.4.refs_1_.refs_0_), channel_id=1, source_target_pairs={{8,0},{9,1},{10,2},{11,3},{12,4},{13,5},{14,6},{15,7},{16,8},{17,9... | collective-permute-start | bytes 3145736 | tf_op jit(solution)/shard_map/ppermute | solution.py:43
  53.7 25.2 %collective-permute-start.3 = (f32[32,8192]{1,0:T(8,128)}, f32[32,8192]{1,0:T(8,128)S(1)}, u32[]{:S(2)}, u32[]{:S(2)}) collective-permute-start(f32[32,8192]{1,0:T(8,128)} %collective-permute-done.2.refs_0_), channel_id=1, source_target_pairs={{8,16},{9,17},{10,18},{11,19},{12,20},{13,21},{14,22},{15,23},{16,... | collective-permute-start | bytes 3145736 | tf_op jit(solution)/shard_map/ppermute | solution.py:43
  54.7 28.1 %collective-permute-start.19 = (f32[32,8192]{1,0:T(8,128)}, f32[32,8192]{1,0:T(8,128)}, u32[]{:S(2)}, u32[]{:S(2)}) collective-permute-start(f32[32,8192]{1,0:T(8,128)} %copy-done.3), channel_id=1, source_target_pairs={{0,1},{1,0},{2,3},{3,2},{4,5},{5,4},{6,7},{7,6},{8,9},{9,8},{10,11... | collective-permute-start | bytes 3145736 | tf_op jit(solution)/shard_map/ppermute | solution.py:43
  60.4 24.4 %collective-permute-start.17 = (f32[32,8192]{1,0:T(8,128)S(1)}, f32[32,8192]{1,0:T(8,128)}, u32[]{:S(2)}, u32[]{:S(2)}) collective-permute-start(f32[32,8192]{1,0:T(8,128)S(1)} %collective-permute-done.4.refs_1_.refs_0_), channel_id=1, source_target_pairs={{0,1},{1,0},{2,3},{3,2},{4,5},{5,4},{6,7},{7,6},{8,9},{9,8},{10,11... | collective-permute-start | bytes 3145736 | tf_op jit(solution)/shard_map/ppermute | solution.py:43
  75.0 12.0 %collective-permute-start.15 = (f32[32,4096]{1,0:T(8,128)}, f32[32,4096]{1,0:T(8,128)}, u32[]{:S(2)}, u32[]{:S(2)}) collective-permute-start(f32[32,4096]{1,0:T(8,128)} %get-tuple-element.37.refs_2_), channel_id=1, source_target_pairs={{0,2},{1,3},{2,0},{3,1},{4,6},{5,7},{6,4},{7,5},{8,10},{9,11},{10,... | collective-permute-start | bytes 1572872 | tf_op jit(solution)/shard_map/ppermute | solution.py:43
  77.6 24.5 %collective-permute-start.7 = (f32[32,8192]{1,0:T(8,128)S(1)}, f32[32,8192]{1,0:T(8,128)}, u32[]{:S(2)}, u32[]{:S(2)}) collective-permute-start(f32[32,8192]{1,0:T(8,128)S(1)} %collective-permute-done.5.refs_2_.refs_1_), channel_id=1, source_target_pairs={{8,0},{9,1},{10,2},{11,3},{12,4},{13,5},{14,6},{15,7}} | collective-permute-start | bytes 3145736 | tf_op jit(solution)/shard_map/ppermute | solution.py:43
  78.9 25.2 %collective-permute-start.6 = (f32[32,8192]{1,0:T(8,128)S(1)}, f32[32,8192]{1,0:T(8,128)}, u32[]{:S(2)}, u32[]{:S(2)}) collective-permute-start(f32[32,8192]{1,0:T(8,128)S(1)} %collective-permute-done.3.refs_1_.refs_0_), channel_id=1, source_target_pairs={{16,24},{17,25},{18,26},{19,27},{20,28},{21,29},{22,30},{23,31}} | collective-permute-start | bytes 3145736 | tf_op jit(solution)/shard_map/ppermute | solution.py:43
  82.8 13.3 %collective-permute-start.16 = (f32[32,4096]{1,0:T(8,128)}, f32[32,4096]{1,0:T(8,128)}, u32[]{:S(2)}, u32[]{:S(2)}) collective-permute-start(f32[32,4096]{1,0:T(8,128)} %get-tuple-element.34.refs_5_), channel_id=1, source_target_pairs={{0,4},{1,5},{2,6},{3,7},{4,0},{5,1},{6,2},{7,3},{8,12},{9,13},{10,... | collective-permute-start | bytes 1572872 | tf_op jit(solution)/shard_map/ppermute | solution.py:43
  84.8 48.8 %collective-permute-start.18 = (f32[32,8192]{1,0:T(8,128)}, f32[32,8192]{1,0:T(8,128)}, u32[]{:S(2)}, u32[]{:S(2)}) collective-permute-start(f32[32,8192]{1,0:T(8,128)} %collective-permute-done.2.refs_0_), channel_id=1, source_target_pairs={{8,9},{9,8},{10,11},{11,10},{12,13},{13,12},{14,15},{15,14},{16,17... | collective-permute-start | bytes 3145736 | tf_op jit(solution)/shard_map/ppermute | solution.py:43
  86.9 64.1 %collective-permute-start.9 = (f32[32,8192]{1,0:T(8,128)S(1)}, f32[32,8192]{1,0:T(8,128)}, u32[]{:S(2)}, u32[]{:S(2)}) collective-permute-start(f32[32,8192]{1,0:T(8,128)S(1)} %collective-permute-done.5.refs_2_.refs_1_), channel_id=1, source_target_pairs={{0,1},{1,0},{2,3},{3,2},{4,5},{5,4},{6,7},{7,6},{8,9},{9,8},{10,11... | collective-permute-start | bytes 3145736 | tf_op jit(solution)/shard_map/ppermute | solution.py:43
  96.1 55.0 %collective-permute-start.8 = (f32[32,8192]{1,0:T(8,128)S(1)}, f32[32,8192]{1,0:T(8,128)}, u32[]{:S(2)}, u32[]{:S(2)}) collective-permute-start(f32[32,8192]{1,0:T(8,128)S(1)} %collective-permute-done.3.refs_1_.refs_0_), channel_id=1, source_target_pairs={{16,17},{17,16},{18,19},{19,18},{20,21},{21,20},{22,23},{23,22},{2... | collective-permute-start | bytes 3145736 | tf_op jit(solution)/shard_map/ppermute | solution.py:43
  102.1 66.4 %collective-permute-start.11 = (f32[32,8192]{1,0:T(8,128)}, f32[32,8192]{1,0:T(8,128)}, u32[]{:S(2)}, u32[]{:S(2)}) collective-permute-start(f32[32,8192]{1,0:T(8,128)} %collective-permute-done.7.refs_3_), channel_id=1, source_target_pairs={{0,1},{1,0},{2,3},{3,2},{4,5},{5,4},{6,7},{7,6}} | collective-permute-start | bytes 3145736 | tf_op jit(solution)/shard_map/ppermute | solution.py:43
  104.1 64.4 %collective-permute-start.10 = (f32[32,8192]{1,0:T(8,128)}, f32[32,8192]{1,0:T(8,128)}, u32[]{:S(2)}, u32[]{:S(2)}) collective-permute-start(f32[32,8192]{1,0:T(8,128)} %collective-permute-done.6.refs_2_), channel_id=1, source_target_pairs={{24,25},{25,24},{26,27},{27,26},{28,29},{29,28},{30,31},{31,30}} | collective-permute-start | bytes 3145736 | tf_op jit(solution)/shard_map/ppermute | solution.py:43
  189.0 5.8 %collective-permute-start.20 = (f32[72,128]{1,0:T(8,128)}, f32[72,128]{1,0:T(8,128)S(1)}, u32[]{:S(2)}, u32[]{:S(2)}) collective-permute-start(f32[72,128]{1,0:T(8,128)} %get-tuple-element.20.refs_0_), channel_id=1, source_target_pairs={{0,4},{1,5},{2,6},{3,7},{4,0},{5,1},{6,2},{7,3},{8,12},{9,13},{10,... | collective-permute-start | bytes 110600 | tf_op jit(solution)/shard_map/ppermute | solution.py:43
  193.3 5.1 %collective-permute-start.22 = (f32[72,128]{1,0:T(8,128)}, f32[72,128]{1,0:T(8,128)S(1)}, u32[]{:S(2)}, u32[]{:S(2)}) collective-permute-start(f32[72,128]{1,0:T(8,128)} %get-tuple-element.20.refs_0_), channel_id=1, source_target_pairs={{0,6},{1,7},{2,4},{3,5},{4,2},{5,3},{6,0},{7,1},{8,14},{9,15},{10,... | collective-permute-start | bytes 110600 | tf_op jit(solution)/shard_map/ppermute | solution.py:43
  213.5 5.1 %collective-permute-start.24 = (f32[72,128]{1,0:T(8,128)}, f32[72,128]{1,0:T(8,128)S(1)}, u32[]{:S(2)}, u32[]{:S(2)}) collective-permute-start(f32[72,128]{1,0:T(8,128)} %join.3.refs_0_), channel_id=1, source_target_pairs={{0,8},{1,9},{2,10},{3,11},{4,12},{5,13},{6,14},{7,15},{8,0},{9,1},... | collective-permute-start | bytes 110600 | tf_op jit(solution)/shard_map/ppermute | solution.py:43
  213.6 6.2 %collective-permute-start.25 = (f32[72,128]{1,0:T(8,128)}, f32[72,128]{1,0:T(8,128)S(1)}, u32[]{:S(2)}, u32[]{:S(2)}) collective-permute-start(f32[72,128]{1,0:T(8,128)} %join.3.refs_0_), channel_id=1, source_target_pairs={{0,16},{1,17},{2,18},{3,19},{4,20},{5,21},{6,22},{7,23},{8,24},{9,... | collective-permute-start | bytes 110600 | tf_op jit(solution)/shard_map/ppermute | solution.py:43
  217.1 6.0 %collective-permute-start.26 = (f32[72,128]{1,0:T(8,128)}, f32[72,128]{1,0:T(8,128)S(1)}, u32[]{:S(2)}, u32[]{:S(2)}) collective-permute-start(f32[72,128]{1,0:T(8,128)} %join.3.refs_0_), channel_id=1, source_target_pairs={{0,24},{1,25},{2,26},{3,27},{4,28},{5,29},{6,30},{7,31},{8,16},{9,... | collective-permute-start | bytes 110600 | tf_op jit(solution)/shard_map/ppermute | solution.py:43
  239.7 5.0 %collective-permute-start.30 = (f32[64,128]{1,0:T(8,128)}, f32[64,128]{1,0:T(8,128)S(1)}, u32[]{:S(2)}, u32[]{:S(2)}) collective-permute-start(f32[64,128]{1,0:T(8,128)} %row_pass.2.refs_0_), channel_id=1, source_target_pairs={{0,6},{1,7},{2,4},{3,5},{4,2},{5,3},{6,0},{7,1},{8,14},{9,15},{10,... | collective-permute-start | bytes 98312 | tf_op jit(solution)/shard_map/ppermute | solution.py:43
  259.9 5.1 %collective-permute-start.33 = (f32[72,128]{1,0:T(8,128)}, f32[72,128]{1,0:T(8,128)S(1)}, u32[]{:S(2)}, u32[]{:S(2)}) collective-permute-start(f32[72,128]{1,0:T(8,128)} %join.4.refs_0_), channel_id=1, source_target_pairs={{0,16},{1,17},{2,18},{3,19},{4,20},{5,21},{6,22},{7,23},{8,24},{9,... | collective-permute-start | bytes 110600 | tf_op jit(solution)/shard_map/ppermute | solution.py:43
  261.0 6.0 %collective-permute-start.34 = (f32[72,128]{1,0:T(8,128)}, f32[72,128]{1,0:T(8,128)S(1)}, u32[]{:S(2)}, u32[]{:S(2)}) collective-permute-start(f32[72,128]{1,0:T(8,128)} %join.4.refs_0_), channel_id=1, source_target_pairs={{0,24},{1,25},{2,26},{3,27},{4,28},{5,29},{6,30},{7,31},{8,16},{9,... | collective-permute-start | bytes 110600 | tf_op jit(solution)/shard_map/ppermute | solution.py:43
  284.7 5.0 %collective-permute-start.38 = (f32[64,128]{1,0:T(8,128)}, f32[64,128]{1,0:T(8,128)S(1)}, u32[]{:S(2)}, u32[]{:S(2)}) collective-permute-start(f32[64,128]{1,0:T(8,128)} %row_pass.3.refs_0_), channel_id=1, source_target_pairs={{0,6},{1,7},{2,4},{3,5},{4,2},{5,3},{6,0},{7,1},{8,14},{9,15},{10,... | collective-permute-start | bytes 98312 | tf_op jit(solution)/shard_map/ppermute | solution.py:43
  304.9 6.0 %collective-permute-start.41 = (f32[72,128]{1,0:T(8,128)}, f32[72,128]{1,0:T(8,128)S(1)}, u32[]{:S(2)}, u32[]{:S(2)}) collective-permute-start(f32[72,128]{1,0:T(8,128)} %join.5.refs_0_), channel_id=1, source_target_pairs={{0,8},{1,9},{2,10},{3,11},{4,12},{5,13},{6,14},{7,15},{8,0},{9,1},... | collective-permute-start | bytes 110600 | tf_op jit(solution)/shard_map/ppermute | solution.py:43
  305.3 5.8 %collective-permute-start.42 = (f32[72,128]{1,0:T(8,128)}, f32[72,128]{1,0:T(8,128)S(1)}, u32[]{:S(2)}, u32[]{:S(2)}) collective-permute-start(f32[72,128]{1,0:T(8,128)} %join.5.refs_0_), channel_id=1, source_target_pairs={{0,16},{1,17},{2,18},{3,19},{4,20},{5,21},{6,22},{7,23},{8,24},{9,... | collective-permute-start | bytes 110600 | tf_op jit(solution)/shard_map/ppermute | solution.py:43
  308.5 6.0 %collective-permute-start.43 = (f32[72,128]{1,0:T(8,128)}, f32[72,128]{1,0:T(8,128)S(1)}, u32[]{:S(2)}, u32[]{:S(2)}) collective-permute-start(f32[72,128]{1,0:T(8,128)} %join.5.refs_0_), channel_id=1, source_target_pairs={{0,24},{1,25},{2,26},{3,27},{4,28},{5,29},{6,30},{7,31},{8,16},{9,... | collective-permute-start | bytes 110600 | tf_op jit(solution)/shard_map/ppermute | solution.py:43
  310.2 8.9 %collective-permute-start.39 = (f32[4096]{0:T(1024)S(1)}, f32[4096]{0:T(1024)S(1)}, u32[]{:S(2)}, u32[]{:S(2)}) collective-permute-start(f32[4096]{0:T(1024)S(1)} %reshape.77), channel_id=1, source_target_pairs={{0,0},{1,4},{2,2},{3,6},{4,1},{5,5},{6,3},{7,7},{8,8},{9,12},{10,1... | collective-permute-start | bytes 49160 | tf_op jit(solution)/shard_map/ppermute | solution.py:43
  (43 other events, 349.5 us)
